TPU v7x, 32 devices: a whole 2x2x4 slice. The times are simulated.
32 devices in a mesh: ctx: 8 (over z, y), exp: 4 (over x, core).
Axes of the slice: x: 2, y: 2, z: 4, core: 2. Of those that a mesh axis runs over, the one named last changes fastest.
Arguments:
- residual: bfloat16 [1024, 6144], P('ctx', 'exp'), may hold values from -6 to 6
- query_rows: bfloat16 [1024, 6144], P('ctx', 'exp'), may hold values from -2 to 2
- key_rows: bfloat16 [1024, 6144], P('ctx', 'exp'), may hold values from -2 to 2
- value_rows: bfloat16 [1024, 6144], P('ctx', 'exp'), may hold values from -6 to 6
- log_decay: float32 [1024, 48], P('ctx', 'exp'), may hold values from -1 to 0
- norm_gain: bfloat16 [6144], P('exp'), may hold values from 0.5 to 1.5
- expert_ids: int32 [1024, 2], P('ctx'), may hold values from 0 to 3, all different within a row; in each aligned block of 128 rows (0 to 127, 128 to 255, ...) at most 96 rows name the same one
- gate_weights: float32 [1024, 2], P('ctx'), may hold values from 0.2 to 1
- w_gate: bfloat16 [4, 6144, 9216], P('exp', None, 'ctx'), may hold values from -0.078125 to 0.078125
- w_up: bfloat16 [4, 6144, 9216], P('exp', None, 'ctx'), may hold values from -0.078125 to 0.078125
- w_down: bfloat16 [4, 9216, 6144], P('exp', 'ctx'), may hold values from -0.0625 to 0.0625
Outputs:
- mixed: bfloat16 [1024, 6144], P('ctx', 'exp')
Inputs may be any that keep to these rules, and one draw needn't show every extreme that they name: `expert_ids`: each token names two different experts; among the 128 tokens of one block at most 96 name any one expert, and in every draw some expert is named by exactly 96 tokens of some block.
All inputs are finite; a program needn't handle non-finite values.
Results may differ from a plain program's by a relative error of at most 0.015.
Values may be sent and summed in bfloat16 or wider, within the bound.
No kernel may reach another device: no remote copies, remote signals or barrier semaphores. Data moves between devices by JAX's collectives and lax.ppermute only.
A program may use at most 128 MiB of HBM per device.

v0:
```python
import jax
import jax.numpy as jnp
from jax import lax
from jax.sharding import PartitionSpec as P

HEAD = 128
precise = lax.Precision.HIGHEST


def from_behind(value, axis, steps):
    count = lax.axis_size(axis)
    initial, last = (max(0, -steps), min(count, count - steps))
    return lax.ppermute(value, axis, [(source, source + steps) for source in range(initial, last)])


def matmul(left, right):
    return jnp.dot(left, right, preferred_element_type=jnp.float32)


def span_parts(query_blk, key_blk, value_blk, decay_blk):
    cumul = jnp.cumsum(decay_blk, axis=0)
    length = decay_blk.shape[0]
    causal = (jnp.arange(length)[:, None] >= jnp.arange(length)[None, :])[:, :, None]
    spread = cumul[:, None, :] - cumul[None, :, :]
    fading = jnp.where(causal, jnp.exp(jnp.where(causal, spread, 0.0)), 0.0)
    query_f = query_blk.astype(jnp.float32)
    key_f = key_blk.astype(jnp.float32)
    value_f = value_blk.astype(jnp.float32)
    scores = jnp.einsum("thd,uhd->htu", query_f, key_f) * jnp.transpose(fading, (2, 0, 1))
    scores = lax.optimization_barrier(scores.astype(jnp.bfloat16))
    inside = jnp.einsum("htu,uhd->thd", scores.astype(jnp.float32), value_f)
    tail = jnp.exp(cumul[-1][None, :] - cumul)
    local = jnp.einsum("uhd,uhe->hde", key_f * tail[:, :, None], value_f, precision=precise)
    return (inside, cumul, query_f, jnp.exp(cumul[-1]), local)


def head_norm(attended, gain):
    meansq = jnp.mean(attended * attended, axis=-1, keepdims=True)
    return attended * lax.rsqrt(meansq + 1e-05) * gain


def per_device(
    residual,
    query_rows,
    key_rows,
    value_rows,
    log_decay,
    norm_gain,
    expert_ids,
    gate_weights,
    w_gate,
    w_up,
    w_down,
):
    token_count, columns = residual.shape
    heads = columns // HEAD
    experts = lax.axis_size("exp")
    capacity = 3 * token_count // experts
    shaped = (token_count, heads, HEAD)
    inside, cumul, query_f, factor, local = span_parts(
        query_rows.reshape(shaped), key_rows.reshape(shaped), value_rows.reshape(shaped), log_decay
    )

    def relay_step(index, incoming):
        total = factor[:, None, None] * incoming + local
        return from_behind(total.astype(jnp.bfloat16), "ctx", 1).astype(total.dtype)

    incoming = lax.fori_loop(0, lax.axis_size("ctx") - 1, relay_step, jnp.zeros_like(local))
    carried = jnp.exp(cumul)[:, :, None] * jnp.einsum(
        "thd,hde->the", query_f, incoming, precision=precise
    )
    attended = inside + carried
    normed = head_norm(attended, norm_gain.astype(jnp.float32).reshape(heads, HEAD)).reshape(
        token_count, columns
    )
    hidden = (residual.astype(jnp.float32) + normed).astype(jnp.bfloat16)
    flat_ids = expert_ids.reshape(2 * token_count)
    onehot = (flat_ids[:, None] == jnp.arange(experts, dtype=jnp.int32)[None, :]).astype(jnp.int32)
    earlier_count = jnp.cumsum(onehot, axis=0) - onehot
    slots = jnp.sum(earlier_count * onehot, axis=1)
    places = flat_ids * capacity + slots
    select = (jnp.arange(experts * capacity, dtype=jnp.int32)[:, None] == places[None, :]).astype(
        jnp.float32
    )
    select = select.reshape(experts * capacity, token_count, 2).sum(axis=2).astype(jnp.bfloat16)
    buckets = matmul(select, hidden).astype(jnp.bfloat16).reshape(experts, capacity, columns)
    arrived = lax.all_to_all(buckets, "exp", split_axis=0, concat_axis=2, tiled=True).reshape(
        capacity, experts * columns
    )
    gate_local = w_gate[0]
    up_local = w_up[0]
    down_local = w_down[0]
    piece = lax.all_gather(arrived, "ctx", axis=0, tiled=True)
    activations = (jax.nn.silu(matmul(piece, gate_local)) * matmul(piece, up_local)).astype(
        jnp.bfloat16
    )
    summed = lax.psum_scatter(
        matmul(activations, down_local).astype(jnp.bfloat16), "ctx", scatter_dimension=0, tiled=True
    )
    expert_out = summed.reshape(1, capacity, experts * columns)
    returned = lax.all_to_all(expert_out, "exp", split_axis=2, concat_axis=0, tiled=True).reshape(
        experts * capacity, columns
    )
    picked = jnp.take(returned, places, axis=0).astype(jnp.float32).reshape(token_count, 2, columns)
    mixed = hidden.astype(jnp.float32) + jnp.sum(gate_weights[:, :, None] * picked, axis=1)
    return mixed.astype(jnp.bfloat16)


def solution(mesh):
    return jax.shard_map(
        per_device,
        mesh=mesh,
        in_specs=(
            P("ctx", "exp"),
            P("ctx", "exp"),
            P("ctx", "exp"),
            P("ctx", "exp"),
            P("ctx", "exp"),
            P("exp"),
            P("ctx", None),
            P("ctx", None),
            P("exp", None, "ctx"),
            P("exp", None, "ctx"),
            P("exp", "ctx", None),
        ),
        out_specs=P("ctx", "exp"),
        check_vma=False,
    )
```

profile of v0, /device:TPU:0, one launch (start us, length us, event | category | flops | bytes accessed | tf_op | source)
XLA Modules:
  0.0 559.8 jit_solution(8698001081078087218)
XLA Ops:
  14.6 81.0 %while.11 = (s32[]{:T(128)}, f32[12,128,128]{2,1,0:T(8,128)S(1)}, f32[12]{0:T(128)S(1)}, f32[12,128,128]{2,1,0:T(8,128)S(1)}, s32[]{:T(128)}, /*index=5*/s32[]{:T(128)}) while((s32[]{:T(128)}, f32[12,128,128]{2,1,0:T(8,128)S(1)}, f32[12]{0:T(128)S(1)}, f32[12,128,128]{2,1,0:T(8,128)S(1)}, s32[]{:T(128)}, /*index=5*/s32[]{:T(128)}) %tuple.25), condition=%wide.region_2.3_spmd.clone, body=%wide.region_1.2_spmd.clone.sunk | while | flops 983043 | bytes 4718759 | solution.py:68
  14.7 4.9 collective-permute-start
  19.7 8.3 %collective-permute-done = bf16[12,128,128]{2,1,0:T(8,128)(2,1)S(1)} collective-permute-done((bf16[12,128,128]{2,1,0:T(8,128)(2,1)S(1)}, bf16[12,128,128]{2,1,0:T(8,128)(2,1)S(1)}, u32[]{:S(2)}, u32[]{:S(2)}) %collective-permute-start) | collective-permute-done | bytes 393248 | tf_op jit(solution)/shard_map/while/body/eval_jaxpr/ppermute | solution.py:13
  32.7 7.5 %collective-permute-done = bf16[12,128,128]{2,1,0:T(8,128)(2,1)S(1)} collective-permute-done((bf16[12,128,128]{2,1,0:T(8,128)(2,1)S(1)}, bf16[12,128,128]{2,1,0:T(8,128)(2,1)S(1)}, u32[]{:S(2)}, u32[]{:S(2)}) %collective-permute-start) | collective-permute-done | bytes 393248 | tf_op jit(solution)/shard_map/while/body/eval_jaxpr/ppermute | solution.py:13
  44.8 6.6 %collective-permute-done = bf16[12,128,128]{2,1,0:T(8,128)(2,1)S(1)} collective-permute-done((bf16[12,128,128]{2,1,0:T(8,128)(2,1)S(1)}, bf16[12,128,128]{2,1,0:T(8,128)(2,1)S(1)}, u32[]{:S(2)}, u32[]{:S(2)}) %collective-permute-start) | collective-permute-done | bytes 393248 | tf_op jit(solution)/shard_map/while/body/eval_jaxpr/ppermute | solution.py:13
  51.7 5.3 collective-permute-start
  57.0 5.8 %collective-permute-done = bf16[12,128,128]{2,1,0:T(8,128)(2,1)S(1)} collective-permute-done((bf16[12,128,128]{2,1,0:T(8,128)(2,1)S(1)}, bf16[12,128,128]{2,1,0:T(8,128)(2,1)S(1)}, u32[]{:S(2)}, u32[]{:S(2)}) %collective-permute-start) | collective-permute-done | bytes 393248 | tf_op jit(solution)/shard_map/while/body/eval_jaxpr/ppermute | solution.py:13
  63.0 5.3 collective-permute-start
  68.3 5.3 collective-permute-done
  73.8 5.3 collective-permute-start
  79.1 5.3 collective-permute-done
  84.6 5.5 collective-permute-start
  90.2 5.3 collective-permute-done
  99.9 18.4 %all_to_all.30 = bf16[4,96,1536]{2,1,0:T(8,128)(2,1)S(1)} all-to-all(bf16[4,96,1536]{2,1,0:T(8,128)(2,1)S(1)} %bitcast.83), channel_id=1, replica_groups=mesh['ctx'=8,'exp'=4] {'exp'}, dimensions={0} | all-to-all | bytes 2359296 | tf_op jit(solution)/shard_map/all_to_all | solution.py:87
  120.7 140.3 %all-gather.2.cloned.1.call-done = bf16[768,6144]{1,0:T(8,128)(2,1)} async-done(((bf16[96,6144]{1,0:T(8,128)(2,1)}), bf16[768,6144]{1,0:T(8,128)(2,1)}) %all-gather.2.cloned.1.call-update) | async-done | bytes 9437200 | tf_op jit(solution)/shard_map/all_gather | solution.py:93
  260.9 16.2 %fusion.6 = f32[768,1152]{1,0:T(8,128)S(1)} fusion(bf16[768,6144]{1,0:T(8,128)(2,1)} %all-gather.2.cloned.1.call-done, bf16[1,6144,1152]{2,1,0:T(8,128)(2,1)} %param.21), kind=kOutput, calls=%fused_computation.8 | convolution fusion | flops 10871635968 | bytes 27131904 | tf_op jit(solution)/shard_map/dot_general | solution.py:17
  277.1 17.1 %fusion.14 = bf16[768,1152]{1,0:T(8,128)(2,1)S(1)} fusion(bf16[768,6144]{1,0:T(8,128)(2,1)} %all-gather.2.cloned.1.call-done, bf16[1,6144,1152]{2,1,0:T(8,128)(2,1)} %param.22, f32[768,1152]{1,0:T(8,128)S(1)} %fusion.6), kind=kOutput, calls=%fused_computation.12 | convolution fusion | flops 10876944384 | bytes 28901376 | tf_op jit(solution)/shard_map/dot_general | solution.py:17
  294.2 14.6 %fusion.8 = bf16[768,6144]{1,0:T(8,128)(2,1)} fusion(bf16[768,1152]{1,0:T(8,128)(2,1)S(1)} %fusion.14, bf16[1,1152,6144]{2,1,0:T(8,128)(2,1)S(1)} %bitcast.100), kind=kOutput, calls=%fused_computation.10 | convolution fusion | flops 10876354560 | bytes 25362432 | tf_op jit(solution)/shard_map/dot_general | solution.py:17
  308.8 160.4 %reduce-scatter.2.cloned.1.call-done = bf16[96,6144]{1,0:T(8,128)(2,1)} async-done(((bf16[768,6144]{1,0:T(8,128)(2,1)}), bf16[96,6144]{1,0:T(8,128)(2,1)}) %reduce-scatter.2.cloned.1.call-update) | async-done | bytes 1179664 | tf_op jit(solution)/shard_map/reduce_scatter | solution.py:97
  469.3 6.7 %copy.139 = bf16[1,96,6144]{1,0,2:T(2,128)(2,1)S(1)} copy(bf16[1,96,6144]{2,1,0:T(8,128)(2,1)} %bitcast.94) | data formatting | bytes 2359296 | tf_op jit(solution)/shard_map/reshape | solution.py:100
  476.5 34.7 %reduce = bf16[6144,96]{1,0:T(8,128)(2,1)} reduce(bf16[6144,1,96]{2,1,0:T(2,128)(2,1)S(1)} %bitcast.80, bf16[]{:T(256)} %broadcast.110), dimensions={1}, to_apply=%bitcast.66.reduce_sub_computation | reduce | bytes 2359298
  511.2 4.8 reshape.169
  522.0 14.1 %all-to-all-done.1 = bf16[4,2,73728]{2,1,0:T(2,128)(2,1)} async-done(((bf16[4,2,73728]{2,1,0:T(2,128)(2,1)}), bf16[4,2,73728]{2,1,0:T(2,128)(2,1)}, u32[]{:S(2)}, u32[]{:S(2)}) %all-to-all-start.1) | async-done | bytes 1179680 | tf_op jit(solution)/shard_map/all_to_all | solution.py:101
  539.7 5.2 copy.140
  (105 shorter events, 43.1 us)
Async XLA Ops:
  6.5 254.4 %all-gather.2.cloned.1.call-start = ((), (), s32[]{:S(2)}) async-start(), calls=%async_computation.3 | async-start | bytes 10616832 | tf_op jit(solution)/shard_map/all_gather | solution.py:93
  14.7 13.3 %collective-permute-start = (bf16[12,128,128]{2,1,0:T(8,128)(2,1)S(1)}, bf16[12,128,128]{2,1,0:T(8,128)(2,1)S(1)}, u32[]{:S(2)}, u32[]{:S(2)}) collective-permute-start(bf16[12,128,128]{2,1,0:T(8,128)(2,1)S(1)} %fusion.44), channel_id=1, source_target_pairs={{0,4},{4,8},{8,12},{12,16},{16,20},{20,24},{24,28},{1,5},{5,9},{9,... | collective-permute-start | bytes 1179656 | tf_op jit(solution)/shard_map/while/body/eval_jaxpr/ppermute | solution.py:13
  28.3 11.9 %collective-permute-start = (bf16[12,128,128]{2,1,0:T(8,128)(2,1)S(1)}, bf16[12,128,128]{2,1,0:T(8,128)(2,1)S(1)}, u32[]{:S(2)}, u32[]{:S(2)}) collective-permute-start(bf16[12,128,128]{2,1,0:T(8,128)(2,1)S(1)} %fusion.44), channel_id=1, source_target_pairs={{0,4},{4,8},{8,12},{12,16},{16,20},{20,24},{24,28},{1,5},{5,9},{9,... | collective-permute-start | bytes 1179656 | tf_op jit(solution)/shard_map/while/body/eval_jaxpr/ppermute | solution.py:13
  40.4 11.0 %collective-permute-start = (bf16[12,128,128]{2,1,0:T(8,128)(2,1)S(1)}, bf16[12,128,128]{2,1,0:T(8,128)(2,1)S(1)}, u32[]{:S(2)}, u32[]{:S(2)}) collective-permute-start(bf16[12,128,128]{2,1,0:T(8,128)(2,1)S(1)} %fusion.44), channel_id=1, source_target_pairs={{0,4},{4,8},{8,12},{12,16},{16,20},{20,24},{24,28},{1,5},{5,9},{9,... | collective-permute-start | bytes 1179656 | tf_op jit(solution)/shard_map/while/body/eval_jaxpr/ppermute | solution.py:13
  51.7 11.0 %collective-permute-start = (bf16[12,128,128]{2,1,0:T(8,128)(2,1)S(1)}, bf16[12,128,128]{2,1,0:T(8,128)(2,1)S(1)}, u32[]{:S(2)}, u32[]{:S(2)}) collective-permute-start(bf16[12,128,128]{2,1,0:T(8,128)(2,1)S(1)} %fusion.44), channel_id=1, source_target_pairs={{0,4},{4,8},{8,12},{12,16},{16,20},{20,24},{24,28},{1,5},{5,9},{9,... | collective-permute-start | bytes 1179656 | tf_op jit(solution)/shard_map/while/body/eval_jaxpr/ppermute | solution.py:13
  63.0 10.6 %collective-permute-start = (bf16[12,128,128]{2,1,0:T(8,128)(2,1)S(1)}, bf16[12,128,128]{2,1,0:T(8,128)(2,1)S(1)}, u32[]{:S(2)}, u32[]{:S(2)}) collective-permute-start(bf16[12,128,128]{2,1,0:T(8,128)(2,1)S(1)} %fusion.44), channel_id=1, source_target_pairs={{0,4},{4,8},{8,12},{12,16},{16,20},{20,24},{24,28},{1,5},{5,9},{9,... | collective-permute-start | bytes 1179656 | tf_op jit(solution)/shard_map/while/body/eval_jaxpr/ppermute | solution.py:13
  73.8 10.6 %collective-permute-start = (bf16[12,128,128]{2,1,0:T(8,128)(2,1)S(1)}, bf16[12,128,128]{2,1,0:T(8,128)(2,1)S(1)}, u32[]{:S(2)}, u32[]{:S(2)}) collective-permute-start(bf16[12,128,128]{2,1,0:T(8,128)(2,1)S(1)} %fusion.44), channel_id=1, source_target_pairs={{0,4},{4,8},{8,12},{12,16},{16,20},{20,24},{24,28},{1,5},{5,9},{9,... | collective-permute-start | bytes 1179656 | tf_op jit(solution)/shard_map/while/body/eval_jaxpr/ppermute | solution.py:13
  84.6 10.8 %collective-permute-start = (bf16[12,128,128]{2,1,0:T(8,128)(2,1)S(1)}, bf16[12,128,128]{2,1,0:T(8,128)(2,1)S(1)}, u32[]{:S(2)}, u32[]{:S(2)}) collective-permute-start(bf16[12,128,128]{2,1,0:T(8,128)(2,1)S(1)} %fusion.44), channel_id=1, source_target_pairs={{0,4},{4,8},{8,12},{12,16},{16,20},{20,24},{24,28},{1,5},{5,9},{9,... | collective-permute-start | bytes 1179656 | tf_op jit(solution)/shard_map/while/body/eval_jaxpr/ppermute | solution.py:13
  95.5 1.3 copy-start.8
  95.5 3.5 copy-start.7
  95.6 3.7 copy-start.4
  95.6 3.8 copy-start.2
  97.4 21.8 %copy-start = (f32[128,1536]{1,0:T(8,128)}, f32[128,1536]{1,0:T(8,128)S(1)}, u32[]{:S(2)}) copy-start(f32[128,1536]{1,0:T(8,128)S(1)} %copy.130) | copy-start | bytes 2359300
  99.1 20.1 %copy-start.5 = (s32[256]{0:T(256)}, s32[256]{0:T(256)S(1)}, u32[]{:S(2)}) copy-start(s32[256]{0:T(256)S(1)} %fusion.27) | copy-start | bytes 3076
  120.4 348.8 %reduce-scatter.2.cloned.1.call-start = ((), (), s32[]{:S(2)}) async-start(), calls=%async_computation.4 | async-start | bytes 10616832 | tf_op jit(solution)/shard_map/reduce_scatter | solution.py:97
  260.9 33.3 %slice-start = ((s8[14155776]{0:T(1024)(128)(4,1)}), s8[4194304]{0:T(1024)(128)(4,1)S(1)}, s32[]{:S(2)}) async-start(s8[14155776]{0:T(1024)(128)(4,1)} %bitcast.99), calls=%async_computation.5 | async-start | bytes 8388608
  260.9 33.3 %slice-start.1 = ((s8[14155776]{0:T(1024)(128)(4,1)}), s8[4194304]{0:T(1024)(128)(4,1)S(1)}, s32[]{:S(2)}) async-start(s8[14155776]{0:T(1024)(128)(4,1)} %bitcast.99), calls=%async_computation.6 | async-start | bytes 8388608
  277.1 17.1 %slice-start.2 = ((s8[14155776]{0:T(1024)(128)(4,1)}), s8[4194304]{0:T(1024)(128)(4,1)S(1)}, s32[]{:S(2)}) async-start(s8[14155776]{0:T(1024)(128)(4,1)} %bitcast.99), calls=%async_computation.7 | async-start | bytes 8388608
  277.1 17.1 %slice-start.3 = ((s8[14155776]{0:T(1024)(128)(4,1)}), s8[1572864]{0:T(1024)(128)(4,1)S(1)}, s32[]{:S(2)}) async-start(s8[14155776]{0:T(1024)(128)(4,1)} %bitcast.99), calls=%async_computation.8 | async-start | bytes 3145728
  511.2 9.5 %copy-start.9 = (f32[128,2]{0,1:T(2,128)S(1)}, f32[128,2]{0,1:T(2,128)}, u32[]{:S(2)}) copy-start(f32[128,2]{0,1:T(2,128)} %param.20) | copy-start | bytes 3076
  511.2 10.2 %copy-start.6 = (s32[256]{0:T(256)S(1)}, s32[256]{0:T(256)}, u32[]{:S(2)}) copy-start(s32[256]{0:T(256)} %copy-done.5) | copy-start | bytes 3076
  516.0 20.2 %all-to-all-start.1 = ((bf16[4,2,73728]{2,1,0:T(2,128)(2,1)}), bf16[4,2,73728]{2,1,0:T(2,128)(2,1)}, u32[]{:S(2)}, u32[]{:S(2)}) async-start(bf16[4,2,73728]{2,1,0:T(2,128)(2,1)} %reshape.169), calls=%async_computation.2 | async-start | bytes 2359296 | tf_op jit(solution)/shard_map/all_to_all | solution.py:101
  547.0 1.9 copy-start.3
  547.0 5.0 copy-start.1
Sparse Core Ops, SparseCore 0:
  120.6 140.3 all-gather.1
  308.9 160.2 reduce-scatter.1
where the time goes:
time: 561 us; the launch traced here: 560 us
  waiting for transfers between devices  359 us (64%)
  matrix products  50.9 us (9%)
  other arithmetic  42.9 us (8%)
  starting transfers between devices  39.7 us (7%)
  local copies, waits for them, and re-layouts  35.1 us (6%)
  blocking collectives  18.4 us (3%)
  between operations  13.8 us (2%)
    reduce_scatter x1, waiting for transfers between devices, per_device(): lax.psum_scatter(matmul(activations, down_local).astype(jnp.bfloat16), 'c...  160 us
    all_gather x1, waiting for transfers between devices, per_device(): piece = lax.all_gather(arrived, 'ctx', axis=0, tiled=True)  140 us
    dot_general x4, matrix products, matmul(): return jnp.dot(left, right, preferred_element_type=jnp.float32)  48.2 us
    ppermute x7, waiting for transfers between devices, from_behind(): lax.ppermute(value, axis, [(source, source + steps) for source in range(i...  43.9 us
    ppermute x7, starting transfers between devices, from_behind(): lax.ppermute(value, axis, [(source, source + steps) for source in range(i...  35.2 us
    unnamed x4, other arithmetic  34.8 us
    all_to_all x1, blocking collectives, per_device(): lax.all_to_all(buckets, 'exp', split_axis=0, concat_axis=2, tiled=True)  18.4 us
    unnamed x38, local copies, waits for them, and re-layouts  16.1 us
  transfers between devices with their start and end apart: 10, of which 10 were waited for; matrix products, arithmetic and copies ran while one was open for 0% of the time, Pallas kernels for 0%

commit v1 on v0

--- a/solution.py
+++ b/solution.py
@@ -98,9 +98,10 @@
         matmul(activations, down_local).astype(jnp.bfloat16), "ctx", scatter_dimension=0, tiled=True
     )
     expert_out = summed.reshape(1, capacity, experts * columns)
-    returned = lax.all_to_all(expert_out, "exp", split_axis=2, concat_axis=0, tiled=True).reshape(
-        experts * capacity, columns
-    )
+    returned = jnp.concatenate(
+        lax.all_to_all(jnp.stack(jnp.split(expert_out, lax.axis_size("exp"), axis=2)), "exp", 0, 0),
+        axis=0,
+    ).reshape(experts * capacity, columns)
     picked = jnp.take(returned, places, axis=0).astype(jnp.float32).reshape(token_count, 2, columns)
     mixed = hidden.astype(jnp.float32) + jnp.sum(gate_weights[:, :, None] * picked, axis=1)
     return mixed.astype(jnp.bfloat16)

time: 561 us -> 504 us (0.90)
  other arithmetic: 42.9 us -> 8.75 us
  local copies, waits for them, and re-layouts: 35.1 us -> 12.6 us
    unnamed x4 -> x3, other arithmetic: 34.8 us -> 0.08 us
    unnamed x38 -> x25, local copies, waits for them, and re-layouts: 16.1 us -> 6.65 us
    all_to_all x3 -> x0, local copies, waits for them, and re-layouts: 7.32 us -> none  [per_device(): lax.all_to_all(expert_out, 'exp', split_axis=2, concat_axis=0, tiled=True)]
    reshape x1 -> x0, local copies, waits for them, and re-layouts: 6.75 us -> none  [per_device(): expert_out = summed.reshape(1, capacity, experts * columns)]
where the time goes in v1:
time: 504 us; the launch traced here: 503 us
  waiting for transfers between devices  360 us (71%)
  matrix products  50.8 us (10%)
  starting transfers between devices  39.1 us (8%)
  blocking collectives  18.4 us (4%)
  between operations  13.7 us (3%)
  local copies, waits for them, and re-layouts  12.6 us (2%)
  other arithmetic  8.75 us (2%)
    reduce_scatter x1, waiting for transfers between devices, per_device(): lax.psum_scatter(matmul(activations, down_local).astype(jnp.bfloat16), 'c...  160 us
    all_gather x1, waiting for transfers between devices, per_device(): piece = lax.all_gather(arrived, 'ctx', axis=0, tiled=True)  140 us
    dot_general x4, matrix products, matmul(): return jnp.dot(left, right, preferred_element_type=jnp.float32)  48.2 us
    ppermute x7, waiting for transfers between devices, from_behind(): lax.ppermute(value, axis, [(source, source + steps) for source in range(i...  43.9 us
    ppermute x7, starting transfers between devices, from_behind(): lax.ppermute(value, axis, [(source, source + steps) for source in range(i...  35.2 us
    all_to_all x1, blocking collectives, per_device(): lax.all_to_all(buckets, 'exp', split_axis=0, concat_axis=2, tiled=True)  18.4 us
    all_to_all x1, waiting for transfers between devices, per_device(): lax.all_to_all(jnp.stack(jnp.split(expert_out, lax.axis_size('exp'), axis...  15 us
  transfers between devices with their start and end apart: 10, of which 10 were waited for; matrix products, arithmetic and copies ran while one was open for 0% of the time, Pallas kernels for 0%

profile of v1, /device:TPU:0, one launch (start us, length us, event | category | flops | bytes accessed | tf_op | source)
XLA Modules:
  0.0 503.3 jit_solution(3229506852879685229)
XLA Ops:
  14.5 80.9 %while.11 = (s32[]{:T(128)}, f32[12,128,128]{2,1,0:T(8,128)S(1)}, f32[12]{0:T(128)S(1)}, f32[12,128,128]{2,1,0:T(8,128)S(1)}, s32[]{:T(128)}, /*index=5*/s32[]{:T(128)}) while((s32[]{:T(128)}, f32[12,128,128]{2,1,0:T(8,128)S(1)}, f32[12]{0:T(128)S(1)}, f32[12,128,128]{2,1,0:T(8,128)S(1)}, s32[]{:T(128)}, /*index=5*/s32[]{:T(128)}) %tuple.28), condition=%wide.region_2.3_spmd.clone, body=%wide.region_1.2_spmd.clone.sunk | while | flops 983043 | bytes 4718759 | solution.py:68
  14.7 4.9 collective-permute-start
  19.6 8.3 %collective-permute-done = bf16[12,128,128]{2,1,0:T(8,128)(2,1)S(1)} collective-permute-done((bf16[12,128,128]{2,1,0:T(8,128)(2,1)S(1)}, bf16[12,128,128]{2,1,0:T(8,128)(2,1)S(1)}, u32[]{:S(2)}, u32[]{:S(2)}) %collective-permute-start) | collective-permute-done | bytes 393248 | tf_op jit(solution)/shard_map/while/body/eval_jaxpr/ppermute | solution.py:13
  28.2 4.4 collective-permute-start
  32.6 7.5 %collective-permute-done = bf16[12,128,128]{2,1,0:T(8,128)(2,1)S(1)} collective-permute-done((bf16[12,128,128]{2,1,0:T(8,128)(2,1)S(1)}, bf16[12,128,128]{2,1,0:T(8,128)(2,1)S(1)}, u32[]{:S(2)}, u32[]{:S(2)}) %collective-permute-start) | collective-permute-done | bytes 393248 | tf_op jit(solution)/shard_map/while/body/eval_jaxpr/ppermute | solution.py:13
  40.4 4.4 collective-permute-start
  44.8 6.6 %collective-permute-done = bf16[12,128,128]{2,1,0:T(8,128)(2,1)S(1)} collective-permute-done((bf16[12,128,128]{2,1,0:T(8,128)(2,1)S(1)}, bf16[12,128,128]{2,1,0:T(8,128)(2,1)S(1)}, u32[]{:S(2)}, u32[]{:S(2)}) %collective-permute-start) | collective-permute-done | bytes 393248 | tf_op jit(solution)/shard_map/while/body/eval_jaxpr/ppermute | solution.py:13
  51.7 5.2 %collective-permute-start = (bf16[12,128,128]{2,1,0:T(8,128)(2,1)S(1)}, bf16[12,128,128]{2,1,0:T(8,128)(2,1)S(1)}, u32[]{:S(2)}, u32[]{:S(2)}) collective-permute-start(bf16[12,128,128]{2,1,0:T(8,128)(2,1)S(1)} %fusion.44), channel_id=1, source_target_pairs={{0,4},{4,8},{8,12},{12,16},{16,20},{20,24},{24,28},{1,5},{5,9},{9,... | collective-permute-start | bytes 1179656 | tf_op jit(solution)/shard_map/while/body/eval_jaxpr/ppermute | solution.py:13
  56.9 5.8 %collective-permute-done = bf16[12,128,128]{2,1,0:T(8,128)(2,1)S(1)} collective-permute-done((bf16[12,128,128]{2,1,0:T(8,128)(2,1)S(1)}, bf16[12,128,128]{2,1,0:T(8,128)(2,1)S(1)}, u32[]{:S(2)}, u32[]{:S(2)}) %collective-permute-start) | collective-permute-done | bytes 393248 | tf_op jit(solution)/shard_map/while/body/eval_jaxpr/ppermute | solution.py:13
  62.9 5.3 %collective-permute-start = (bf16[12,128,128]{2,1,0:T(8,128)(2,1)S(1)}, bf16[12,128,128]{2,1,0:T(8,128)(2,1)S(1)}, u32[]{:S(2)}, u32[]{:S(2)}) collective-permute-start(bf16[12,128,128]{2,1,0:T(8,128)(2,1)S(1)} %fusion.44), channel_id=1, source_target_pairs={{0,4},{4,8},{8,12},{12,16},{16,20},{20,24},{24,28},{1,5},{5,9},{9,... | collective-permute-start | bytes 1179656 | tf_op jit(solution)/shard_map/while/body/eval_jaxpr/ppermute | solution.py:13
  68.2 5.3 %collective-permute-done = bf16[12,128,128]{2,1,0:T(8,128)(2,1)S(1)} collective-permute-done((bf16[12,128,128]{2,1,0:T(8,128)(2,1)S(1)}, bf16[12,128,128]{2,1,0:T(8,128)(2,1)S(1)}, u32[]{:S(2)}, u32[]{:S(2)}) %collective-permute-start) | collective-permute-done | bytes 393248 | tf_op jit(solution)/shard_map/while/body/eval_jaxpr/ppermute | solution.py:13
  73.7 5.3 %collective-permute-start = (bf16[12,128,128]{2,1,0:T(8,128)(2,1)S(1)}, bf16[12,128,128]{2,1,0:T(8,128)(2,1)S(1)}, u32[]{:S(2)}, u32[]{:S(2)}) collective-permute-start(bf16[12,128,128]{2,1,0:T(8,128)(2,1)S(1)} %fusion.44), channel_id=1, source_target_pairs={{0,4},{4,8},{8,12},{12,16},{16,20},{20,24},{24,28},{1,5},{5,9},{9,... | collective-permute-start | bytes 1179656 | tf_op jit(solution)/shard_map/while/body/eval_jaxpr/ppermute | solution.py:13
  79.1 5.3 %collective-permute-done = bf16[12,128,128]{2,1,0:T(8,128)(2,1)S(1)} collective-permute-done((bf16[12,128,128]{2,1,0:T(8,128)(2,1)S(1)}, bf16[12,128,128]{2,1,0:T(8,128)(2,1)S(1)}, u32[]{:S(2)}, u32[]{:S(2)}) %collective-permute-start) | collective-permute-done | bytes 393248 | tf_op jit(solution)/shard_map/while/body/eval_jaxpr/ppermute | solution.py:13
  84.6 5.6 %collective-permute-start = (bf16[12,128,128]{2,1,0:T(8,128)(2,1)S(1)}, bf16[12,128,128]{2,1,0:T(8,128)(2,1)S(1)}, u32[]{:S(2)}, u32[]{:S(2)}) collective-permute-start(bf16[12,128,128]{2,1,0:T(8,128)(2,1)S(1)} %fusion.44), channel_id=1, source_target_pairs={{0,4},{4,8},{8,12},{12,16},{16,20},{20,24},{24,28},{1,5},{5,9},{9,... | collective-permute-start | bytes 1179656 | tf_op jit(solution)/shard_map/while/body/eval_jaxpr/ppermute | solution.py:13
  90.1 5.3 %collective-permute-done = bf16[12,128,128]{2,1,0:T(8,128)(2,1)S(1)} collective-permute-done((bf16[12,128,128]{2,1,0:T(8,128)(2,1)S(1)}, bf16[12,128,128]{2,1,0:T(8,128)(2,1)S(1)}, u32[]{:S(2)}, u32[]{:S(2)}) %collective-permute-start) | collective-permute-done | bytes 393248 | tf_op jit(solution)/shard_map/while/body/eval_jaxpr/ppermute | solution.py:13
  99.8 18.4 %all_to_all.20 = bf16[4,96,1536]{2,1,0:T(8,128)(2,1)S(1)} all-to-all(bf16[4,96,1536]{2,1,0:T(8,128)(2,1)S(1)} %bitcast.86), channel_id=1, replica_groups=mesh['ctx'=8,'exp'=4] {'exp'}, dimensions={0} | all-to-all | bytes 2359296 | tf_op jit(solution)/shard_map/all_to_all | solution.py:87
  120.5 140.2 %all-gather.2.cloned.1.call-done = bf16[768,6144]{1,0:T(8,128)(2,1)} async-done(((bf16[96,6144]{1,0:T(8,128)(2,1)}), bf16[768,6144]{1,0:T(8,128)(2,1)}) %all-gather.2.cloned.1.call-update) | async-done | bytes 9437200 | tf_op jit(solution)/shard_map/all_gather | solution.py:93
  260.8 16.1 %fusion.6 = f32[768,1152]{1,0:T(8,128)S(1)} fusion(bf16[768,6144]{1,0:T(8,128)(2,1)} %all-gather.2.cloned.1.call-done, bf16[1,6144,1152]{2,1,0:T(8,128)(2,1)} %param.21), kind=kOutput, calls=%fused_computation.8 | convolution fusion | flops 10871635968 | bytes 27131904 | tf_op jit(solution)/shard_map/dot_general | solution.py:17
  277.0 17.1 %fusion.14 = bf16[768,1152]{1,0:T(8,128)(2,1)S(1)} fusion(bf16[768,6144]{1,0:T(8,128)(2,1)} %all-gather.2.cloned.1.call-done, bf16[1,6144,1152]{2,1,0:T(8,128)(2,1)} %param.22, f32[768,1152]{1,0:T(8,128)S(1)} %fusion.6), kind=kOutput, calls=%fused_computation.12 | convolution fusion | flops 10876944384 | bytes 28901376 | tf_op jit(solution)/shard_map/dot_general | solution.py:17
  294.1 14.5 %fusion.8 = bf16[768,6144]{1,0:T(8,128)(2,1)} fusion(bf16[768,1152]{1,0:T(8,128)(2,1)S(1)} %fusion.14, bf16[1,1152,6144]{2,1,0:T(8,128)(2,1)S(1)} %bitcast.102), kind=kOutput, calls=%fused_computation.10 | convolution fusion | flops 10876354560 | bytes 25362432 | tf_op jit(solution)/shard_map/dot_general | solution.py:17
  308.6 160.4 %reduce-scatter.2.cloned.1.call-done = bf16[96,6144]{1,0:T(8,128)(2,1)} async-done(((bf16[768,6144]{1,0:T(8,128)(2,1)}), bf16[96,6144]{1,0:T(8,128)(2,1)}) %reduce-scatter.2.cloned.1.call-update) | async-done | bytes 1179664 | tf_op jit(solution)/shard_map/reduce_scatter | solution.py:97
  471.5 3.7 all-to-all-start.1
  475.8 15.0 %all-to-all-done.1 = bf16[4,1,96,1536]{3,2,1,0:T(8,128)(2,1)S(1)} async-done(((bf16[4,1,96,1536]{3,2,1,0:T(8,128)(2,1)}), bf16[4,1,96,1536]{3,2,1,0:T(8,128)(2,1)S(1)}, u32[]{:S(2)}, u32[]{:S(2)}) %all-to-all-start.1) | async-done | bytes 1179680 | tf_op jit(solution)/shard_map/all_to_all | solution.py:102
  492.4 3.2 multiply_reduce_fusion
  (89 shorter events, 21.5 us)
Async XLA Ops:
  6.5 254.2 %all-gather.2.cloned.1.call-start = ((), (), s32[]{:S(2)}) async-start(), calls=%async_computation.3 | async-start | bytes 10616832 | tf_op jit(solution)/shard_map/all_gather | solution.py:93
  14.7 13.3 %collective-permute-start = (bf16[12,128,128]{2,1,0:T(8,128)(2,1)S(1)}, bf16[12,128,128]{2,1,0:T(8,128)(2,1)S(1)}, u32[]{:S(2)}, u32[]{:S(2)}) collective-permute-start(bf16[12,128,128]{2,1,0:T(8,128)(2,1)S(1)} %fusion.44), channel_id=1, source_target_pairs={{0,4},{4,8},{8,12},{12,16},{16,20},{20,24},{24,28},{1,5},{5,9},{9,... | collective-permute-start | bytes 1179656 | tf_op jit(solution)/shard_map/while/body/eval_jaxpr/ppermute | solution.py:13
  28.2 11.9 %collective-permute-start = (bf16[12,128,128]{2,1,0:T(8,128)(2,1)S(1)}, bf16[12,128,128]{2,1,0:T(8,128)(2,1)S(1)}, u32[]{:S(2)}, u32[]{:S(2)}) collective-permute-start(bf16[12,128,128]{2,1,0:T(8,128)(2,1)S(1)} %fusion.44), channel_id=1, source_target_pairs={{0,4},{4,8},{8,12},{12,16},{16,20},{20,24},{24,28},{1,5},{5,9},{9,... | collective-permute-start | bytes 1179656 | tf_op jit(solution)/shard_map/while/body/eval_jaxpr/ppermute | solution.py:13
  40.4 11.0 %collective-permute-start = (bf16[12,128,128]{2,1,0:T(8,128)(2,1)S(1)}, bf16[12,128,128]{2,1,0:T(8,128)(2,1)S(1)}, u32[]{:S(2)}, u32[]{:S(2)}) collective-permute-start(bf16[12,128,128]{2,1,0:T(8,128)(2,1)S(1)} %fusion.44), channel_id=1, source_target_pairs={{0,4},{4,8},{8,12},{12,16},{16,20},{20,24},{24,28},{1,5},{5,9},{9,... | collective-permute-start | bytes 1179656 | tf_op jit(solution)/shard_map/while/body/eval_jaxpr/ppermute | solution.py:13
  51.7 11.0 %collective-permute-start = (bf16[12,128,128]{2,1,0:T(8,128)(2,1)S(1)}, bf16[12,128,128]{2,1,0:T(8,128)(2,1)S(1)}, u32[]{:S(2)}, u32[]{:S(2)}) collective-permute-start(bf16[12,128,128]{2,1,0:T(8,128)(2,1)S(1)} %fusion.44), channel_id=1, source_target_pairs={{0,4},{4,8},{8,12},{12,16},{16,20},{20,24},{24,28},{1,5},{5,9},{9,... | collective-permute-start | bytes 1179656 | tf_op jit(solution)/shard_map/while/body/eval_jaxpr/ppermute | solution.py:13
  62.9 10.6 %collective-permute-start = (bf16[12,128,128]{2,1,0:T(8,128)(2,1)S(1)}, bf16[12,128,128]{2,1,0:T(8,128)(2,1)S(1)}, u32[]{:S(2)}, u32[]{:S(2)}) collective-permute-start(bf16[12,128,128]{2,1,0:T(8,128)(2,1)S(1)} %fusion.44), channel_id=1, source_target_pairs={{0,4},{4,8},{8,12},{12,16},{16,20},{20,24},{24,28},{1,5},{5,9},{9,... | collective-permute-start | bytes 1179656 | tf_op jit(solution)/shard_map/while/body/eval_jaxpr/ppermute | solution.py:13
  73.7 10.6 %collective-permute-start = (bf16[12,128,128]{2,1,0:T(8,128)(2,1)S(1)}, bf16[12,128,128]{2,1,0:T(8,128)(2,1)S(1)}, u32[]{:S(2)}, u32[]{:S(2)}) collective-permute-start(bf16[12,128,128]{2,1,0:T(8,128)(2,1)S(1)} %fusion.44), channel_id=1, source_target_pairs={{0,4},{4,8},{8,12},{12,16},{16,20},{20,24},{24,28},{1,5},{5,9},{9,... | collective-permute-start | bytes 1179656 | tf_op jit(solution)/shard_map/while/body/eval_jaxpr/ppermute | solution.py:13
  84.6 10.8 %collective-permute-start = (bf16[12,128,128]{2,1,0:T(8,128)(2,1)S(1)}, bf16[12,128,128]{2,1,0:T(8,128)(2,1)S(1)}, u32[]{:S(2)}, u32[]{:S(2)}) collective-permute-start(bf16[12,128,128]{2,1,0:T(8,128)(2,1)S(1)} %fusion.44), channel_id=1, source_target_pairs={{0,4},{4,8},{8,12},{12,16},{16,20},{20,24},{24,28},{1,5},{5,9},{9,... | collective-permute-start | bytes 1179656 | tf_op jit(solution)/shard_map/while/body/eval_jaxpr/ppermute | solution.py:13
  95.5 1.3 copy-start.3
  95.5 3.5 copy-start.2
  95.5 3.7 copy-start.1
  95.5 3.8 copy-start
  120.3 348.7 %reduce-scatter.2.cloned.1.call-start = ((), (), s32[]{:S(2)}) async-start(), calls=%async_computation.4 | async-start | bytes 10616832 | tf_op jit(solution)/shard_map/reduce_scatter | solution.py:97
  260.8 33.2 %slice-start = ((s8[14155776]{0:T(1024)(128)(4,1)}), s8[4194304]{0:T(1024)(128)(4,1)S(1)}, s32[]{:S(2)}) async-start(s8[14155776]{0:T(1024)(128)(4,1)} %bitcast.101), calls=%async_computation.5 | async-start | bytes 8388608
  260.8 33.3 %slice-start.1 = ((s8[14155776]{0:T(1024)(128)(4,1)}), s8[4194304]{0:T(1024)(128)(4,1)S(1)}, s32[]{:S(2)}) async-start(s8[14155776]{0:T(1024)(128)(4,1)} %bitcast.101), calls=%async_computation.6 | async-start | bytes 8388608
  276.9 17.1 %slice-start.2 = ((s8[14155776]{0:T(1024)(128)(4,1)}), s8[4194304]{0:T(1024)(128)(4,1)S(1)}, s32[]{:S(2)}) async-start(s8[14155776]{0:T(1024)(128)(4,1)} %bitcast.101), calls=%async_computation.7 | async-start | bytes 8388608
  276.9 17.1 %slice-start.3 = ((s8[14155776]{0:T(1024)(128)(4,1)}), s8[1572864]{0:T(1024)(128)(4,1)S(1)}, s32[]{:S(2)}) async-start(s8[14155776]{0:T(1024)(128)(4,1)} %bitcast.101), calls=%async_computation.8 | async-start | bytes 3145728
  469.0 6.7 %copy-start.4 = (f32[128,2]{0,1:T(2,128)S(1)}, f32[128,2]{0,1:T(2,128)}, u32[]{:S(2)}) copy-start(f32[128,2]{0,1:T(2,128)} %param.20) | copy-start | bytes 3076
  471.5 19.3 %all-to-all-start.1 = ((bf16[4,1,96,1536]{3,2,1,0:T(8,128)(2,1)}), bf16[4,1,96,1536]{3,2,1,0:T(8,128)(2,1)S(1)}, u32[]{:S(2)}, u32[]{:S(2)}) async-start(bf16[4,1,96,1536]{3,2,1,0:T(8,128)(2,1)} %pad_maximum_fusion), calls=%async_computation.2 | async-start | bytes 2359296 | tf_op jit(solution)/shard_map/all_to_all | solution.py:102
Sparse Core Ops, SparseCore 0:
  120.4 140.3 all-gather.1
  308.7 160.2 reduce-scatter.1
